TPU v7x, 32 devices: a whole 2x2x4 slice. The times are simulated.
32 devices in a mesh: boot: 4 (over z), tm: 8 (over y, x, core).
Axes of the slice: x: 2, y: 2, z: 4, core: 2. Of those that a mesh axis runs over, the one named last changes fastest.
Arguments:
- recording: bfloat16 [4096, 1024], P('tm'), may hold values from -60 to 60, as said below
- starts: int32 [4, 48], P('boot', 'tm'), may hold values from 0 to 448, as said below
- lengths: int32 [4, 48], P('boot', 'tm'), may hold values from 1 to 64, as said below
- support: int32 [4, 4096], P(None, 'boot'), may hold values 0 or 1
Outputs:
- averaged: float32 [32, 4096], P(None, 'boot')
- residual: float32 [32, 4096], P(None, 'tm')
Inputs may be any that keep to these rules, and one draw needn't show every extreme that they name: A shard's values are an autoregressive recording; its values stay within the range. Entry [b, j * 6 + k] starts block k of resample b on time shard j, counted from the shard's first sample; a block ends inside its shard. The 6 lengths of one resample on one time shard sum to at most 384.
All inputs are finite; a program needn't handle non-finite values. No bound on the sum of `support` on one device may be relied on, other than what follows from the above.
Results may differ from a plain program's by a relative error of at most 0.0043.
The roundings to bfloat16 on the way count: a program that leaves them out, or rounds other values in their place, can miss the bound.
Values may be sent and summed in bfloat16 or wider, within the bound.
No kernel may reach another device: no remote copies, remote signals or barrier semaphores. Data moves between devices by JAX's collectives and lax.ppermute only.
A program may use at most 64 MiB of HBM per device.

v0:
```python
import jax
import jax.numpy as jnp
from jax import lax
from jax.sharding import PartitionSpec as P

CHANNEL_COUNT = 1024
LAGS = 4
RESPONSE_COUNT = 32
NBLK = 6
CAP = 384
ITERS = 3
CHEB = 5
ridge_weight = 4.0
shrink_level = 0.75
epsilon = 1e-05


def passed_along(block, axis, distance):
    devices = range(lax.axis_size(axis))
    route = [(i - distance, i) for i in devices if i - distance in devices]
    return lax.ppermute(block, axis, route)


def bootstrap_rows(window, begins, sizes):
    ends = jnp.cumsum(sizes)
    offsets = ends - sizes
    total = ends[-1]
    rows = jnp.arange(CAP, dtype=jnp.int32)
    member = (rows[:, None] >= offsets[None, :]).astype(jnp.int32)
    which = jnp.sum(member, axis=1) - 1
    picked = (which[:, None] == jnp.arange(NBLK, dtype=jnp.int32)[None, :]).astype(jnp.int32)
    anchor = jnp.sum(picked * offsets[None, :], axis=1)
    opening = jnp.sum(picked * begins[None, :], axis=1)
    live = rows < total
    times = jnp.where(live, opening + rows - anchor, 0)
    blocks = [jnp.take(window, times + LAGS - 1 - delay_step, axis=0) for delay_step in range(LAGS)]
    design = jnp.concatenate(blocks, axis=1)
    design = jnp.where(live[:, None], design, jnp.zeros_like(design))
    answer = jnp.take(window[:, :RESPONSE_COUNT], times + LAGS, axis=0)
    answer = jnp.where(live[:, None], answer, jnp.zeros_like(answer))
    return (design, answer.T)


def chebyshev(gram, rhs, bound):
    center = ridge_weight + 0.5 * bound
    radius = 0.5 * bound
    sigma = center / radius
    solution = jnp.zeros_like(rhs)
    remain = rhs
    factor = 1.0 / sigma
    update = rhs / center
    for count in range(CHEB):
        solution = solution + update
        if count + 1 < CHEB:
            applied = ridge_weight * update + jnp.einsum(
                "brc,bcd->brd", update, gram, precision=lax.Precision.HIGHEST
            )
            remain = remain - applied
            after = 1.0 / (2.0 * sigma - factor)
            update = after * factor * update + 2.0 * after / radius * remain
            factor = after
    return solution


def shrink_columns(mean_value, norms, level):
    return mean_value * (jnp.maximum(norms - level, 0.0) / jnp.maximum(norms, level))[:, None, :]


def per_device(recording, starts, lengths, support):
    shards = lax.axis_size("tm")
    samples = recording.shape[0]
    values = recording.astype(jnp.float32)
    power = lax.psum(jnp.sum(values * values, axis=0), "tm")
    scale = 1.0 / jnp.sqrt(power / (samples * shards) + epsilon)
    scaled_input = (values * scale).astype(jnp.bfloat16)
    carried = passed_along(scaled_input[samples - LAGS :], "tm", 1)
    extended = jnp.concatenate([carried, scaled_input], axis=0)
    design, answer = jax.vmap(bootstrap_rows, in_axes=(None, 0, 0))(extended, starts, lengths)
    row_scale = 1.0 / CAP
    cross = (
        jnp.einsum("brc,bcf->brf", answer, design, preferred_element_type=jnp.float32) * row_scale
    )
    gram = (
        jnp.einsum("bcf,bdf->bcd", design, design, preferred_element_type=jnp.float32) * row_scale
    )
    bound = jnp.sqrt(jnp.sum(gram * gram, axis=(1, 2)))[:, None, None]
    consensus = jnp.zeros_like(cross)
    dual = jnp.zeros_like(cross)
    for rounds in range(ITERS):
        target = cross + ridge_weight * (consensus - dual)
        projected = (
            jnp.einsum(
                "brf,bcf->brc",
                target.astype(jnp.bfloat16),
                design,
                preferred_element_type=jnp.float32,
            )
            * row_scale
        )
        weights = chebyshev(gram, projected, bound)
        back = jnp.einsum(
            "brc,bcf->brf", weights.astype(jnp.bfloat16), design, preferred_element_type=jnp.float32
        )
        local = (target - back) / ridge_weight
        stacked = local + dual
        mean_value = lax.psum(stacked, "tm") / shards
        norms = jnp.sqrt(jnp.sum(mean_value * mean_value, axis=1))
        level = shrink_level * jnp.mean(norms, axis=1, keepdims=True)
        consensus = shrink_columns(mean_value, norms, level)
        dual = dual + local - consensus
    width = consensus.shape[2] // lax.axis_size("boot")
    position = lax.axis_index("boot")
    chosen = support.astype(jnp.float32)
    tally = jnp.sum(chosen, axis=0)
    mine = lax.all_to_all(support, "boot", split_axis=0, concat_axis=1, tiled=True).astype(
        jnp.float32
    )
    weighted = jnp.sum(mine[:, None, :] * consensus, axis=0)
    summed = lax.psum_scatter(weighted, "boot", scatter_dimension=1, tiled=True)
    averaged = summed / jnp.maximum(tally, 1.0)[None, :]
    opening = position * width
    delay_step = opening // CHANNEL_COUNT
    channel = opening % CHANNEL_COUNT
    columns = lax.dynamic_slice(extended, (LAGS - 1 - delay_step, channel), (samples, width))
    partial_result = lax.dot_general(
        averaged.astype(jnp.bfloat16),
        columns,
        (((1,), (1,)), ((), ())),
        preferred_element_type=jnp.float32,
    )
    predicted_output = lax.psum(partial_result, "boot")
    residual = scaled_input[:, :RESPONSE_COUNT].astype(jnp.float32).T - predicted_output
    return (averaged, residual)


def solution(mesh):
    in_specs = (P("tm", None), P("boot", "tm"), P("boot", "tm"), P(None, "boot"))
    out_specs = (P(None, "boot"), P(None, "tm"))
    return jax.shard_map(
        per_device, mesh=mesh, in_specs=in_specs, out_specs=out_specs, check_vma=False
    )
```

profile of v0, /device:TPU:0, one launch (start us, length us, event | category | flops | bytes accessed | tf_op | source)
XLA Modules:
  0.0 315.7 jit_solution(589085711330140276)
XLA Ops:
  7.2 1.5 copy.24
  9.0 15.2 %psum.35 = f32[1024]{0:T(1024)S(1)} all-reduce(f32[1024]{0:T(1024)S(1)} %fusion.9), channel_id=1, replica_groups=mesh['boot'=4,'tm'=8] {'tm'}, use_global_device_ids=true, to_apply=%region_5.6 | all-reduce | flops 1024 | bytes 8192 | tf_op jit(solution)/shard_map/psum | solution.py:73
  24.6 1.3 collective-permute-start
  26.1 0.6 slice.12
  26.9 0.7 iota_compare_fusion
  27.6 0.7 fusion.114
  28.3 0.7 and_reduce_fusion.3
  29.1 0.7 copy-done.10
  29.8 0.7 pad_maximum_fusion
  30.5 0.6 copy.26
  31.1 2.7 gather_fusion.4
  33.8 2.7 gather_fusion.3
  36.5 2.7 gather_fusion.2
  39.2 2.7 gather_fusion.1
  41.9 2.7 fusion.38
  44.5 1.4 fusion.42
  45.9 0.9 fusion.8
  46.8 2.5 multiply_reduce_fusion
  50.7 1.4 gather_fusion
  52.1 2.7 convolution_multiply_fusion
  54.8 2.1 maximum_select_fusion.1
  56.9 1.0 convolution_multiply_fusion.4
  58.8 0.4 fusion.29
  59.3 0.4 fusion.32
  59.7 1.5 fusion.1
  61.5 58.2 %all-reduce.5.cloned.1.call-done = f32[1,32,4096]{2,1,0:T(8,128)} async-done(((f32[1,32,4096]{2,1,0:T(8,128)}), f32[1,32,4096]{2,1,0:T(8,128)}) %all-reduce.5.cloned.1.call-update) | async-done | bytes 524304 | tf_op jit(solution)/shard_map/psum | solution.py:106
  119.7 1.1 multiply_reduce_fusion.3
  120.8 0.7 sqrt_reduce_fusion.2
  122.1 3.4 %convolution_multiply_fusion.3 = f32[32,384]{1,0:T(8,128)S(1)} fusion(bf16[384,4096]{1,0:T(8,128)(2,1)} %copy-done.3, f32[1,32,4096]{2,1,0:T(8,128)} %fusion.1, f32[1,32,4096]{2,1,0:T(8,128)} %all-reduce.5.cloned.1.call-done, f32[32,4096]{1,0:T(8,128)S(1)} %convolution_multiply_fusion, f32[4096]{0:T(1024)S(1)} %divide_multiply_fusion.2), kind=kOutput, calls=%fused_computation.31 | convolution fusion | flops 101462016 | bytes 4784128 | tf_op jit(solution)/shard_map/brf,bcf->brc/dot_general | solution.py:92
  126.8 0.4 fusion.33
  127.3 1.5 fusion.7
  129.0 54.2 %all-reduce.7.cloned.1.call-done = f32[1,32,4096]{2,1,0:T(8,128)} async-done(((f32[1,32,4096]{2,1,0:T(8,128)}), f32[1,32,4096]{2,1,0:T(8,128)}) %all-reduce.7.cloned.1.call-update) | async-done | bytes 524304 | tf_op jit(solution)/shard_map/psum | solution.py:106
  183.2 1.1 multiply_reduce_fusion.2
  184.3 0.7 sqrt_reduce_fusion.1
  185.6 3.4 %convolution_multiply_fusion.2 = f32[32,384]{1,0:T(8,128)S(1)} fusion(bf16[384,4096]{1,0:T(8,128)(2,1)} %copy-done.3, f32[1,32,4096]{2,1,0:T(8,128)} %fusion.7, f32[1,32,4096]{2,1,0:T(8,128)} %all-reduce.7.cloned.1.call-done, f32[32,4096]{1,0:T(8,128)S(1)} %convolution_multiply_fusion, f32[4096]{0:T(1024)S(1)} %divide_multiply_fusion.1), kind=kOutput, calls=%fused_computation.30 | convolution fusion | flops 101462016 | bytes 4784128 | tf_op jit(solution)/shard_map/brf,bcf->brc/dot_general | solution.py:92
  189.9 0.4 fusion.15
  190.4 0.4 fusion.34
  190.9 1.5 fusion.4
  192.5 9.9 %all_to_all.13 = s32[4,1,1024]{2,1,0:T(1,128)S(1)} all-to-all(s32[4,1,1024]{2,1,0:T(1,128)S(1)} %all_to_all.10), channel_id=1, replica_groups=mesh['boot'=4,'tm'=8] {'boot'}, dimensions={0} | all-to-all | bytes 32768 | tf_op jit(solution)/shard_map/all_to_all | solution.py:115
  202.5 44.2 %all-reduce.9.cloned.1.call-done = f32[1,32,4096]{2,1,0:T(8,128)} async-done(((f32[1,32,4096]{2,1,0:T(8,128)}), f32[1,32,4096]{2,1,0:T(8,128)}) %all-reduce.9.cloned.1.call-update) | async-done | bytes 524304 | tf_op jit(solution)/shard_map/psum | solution.py:106
  246.7 1.1 multiply_reduce_fusion.1
  247.8 0.6 sqrt_reduce_fusion
  249.1 1.9 multiply_bitcast_fusion
  251.1 21.2 %reduce-scatter.2.cloned.1.call-done = f32[32,1024]{1,0:T(8,128)} async-done(((f32[32,4096]{1,0:T(8,128)}), f32[32,1024]{1,0:T(8,128)}) %reduce-scatter.2.cloned.1.call-update) | async-done | bytes 131088 | tf_op jit(solution)/shard_map/reduce_scatter | solution.py:119
  272.4 0.9 broadcast_divide_fusion
  273.3 1.3 fusion.36
  274.6 33.1 %all-reduce.11.cloned.1.call-done = f32[32,512]{1,0:T(8,128)} async-done(((f32[32,512]{1,0:T(8,128)}), f32[32,512]{1,0:T(8,128)}) %all-reduce.11.cloned.1.call-update) | async-done | bytes 65552 | tf_op jit(solution)/shard_map/psum | solution.py:131
  307.7 1.5 bitcast_subtract_fusion
  (73 shorter events, 5.0 us)
Async XLA Ops:
  7.2 18.8 %copy-start.15 = (s32[1,6]{1,0:T(1,128)S(1)}, s32[1,6]{1,0:T(1,128)}, u32[]{:S(2)}) copy-start(s32[1,6]{1,0:T(1,128)} %param.8) | copy-start | bytes 76
  7.2 19.6 %copy-start.14 = (s32[1,6]{1,0:T(1,128)S(1)}, s32[1,6]{1,0:T(1,128)}, u32[]{:S(2)}) copy-start(s32[1,6]{1,0:T(1,128)} %param.7) | copy-start | bytes 76
  7.2 112.5 %all-reduce.5.cloned.1.call-start = ((), (), s32[]{:S(2)}) async-start(), calls=%async_computation.2 | async-start | bytes 1048576 | tf_op jit(solution)/shard_map/psum | solution.py:106
  24.6 4.4 %collective-permute-start = (bf16[4,1024]{0,1:T(8,128)(2,1)S(1)}, bf16[4,1024]{0,1:T(8,128)(2,1)S(1)}, u32[]{:S(2)}, u32[]{:S(2)}) collective-permute-start(bf16[4,1024]{0,1:T(8,128)(2,1)S(1)} %slice.26), channel_id=1, source_target_pairs={{0,1},{1,2},{2,3},{3,4},{4,5},{5,6},{6,7},{8,9},{9,10},{10,11},{11... | collective-permute-start | bytes 24584 | tf_op jit(solution)/shard_map/ppermute | solution.py:21
  29.1 0.7 copy-start.10
  41.9 2.7 copy-start.8
  41.9 2.7 copy-start.9
  46.8 2.5 copy-start.3
  46.8 3.4 %copy-start.11 = (bf16[4,1024]{0,1:T(8,128)(2,1)S(1)}, bf16[4,1024]{0,1:T(8,128)(2,1)}, u32[]{:S(2)}) copy-start(bf16[4,1024]{0,1:T(8,128)(2,1)} %copy-done.10) | copy-start | bytes 24580
  56.9 2.8 copy-start
  61.3 121.9 %all-reduce.7.cloned.1.call-start = ((), (), s32[]{:S(2)}) async-start(), calls=%async_computation.3 | async-start | bytes 1048576 | tf_op jit(solution)/shard_map/psum | solution.py:106
  122.1 5.2 %copy-start.1 = (bf16[384,4096]{1,0:T(8,128)(2,1)S(1)}, bf16[384,4096]{1,0:T(8,128)(2,1)}, u32[]{:S(2)}) copy-start(bf16[384,4096]{1,0:T(8,128)(2,1)} %copy-done) | copy-start | bytes 9437188
  122.1 5.2 %copy-start.5 = (f32[1,32,4096]{2,1,0:T(8,128)S(1)}, f32[1,32,4096]{2,1,0:T(8,128)}, u32[]{:S(2)}) copy-start(f32[1,32,4096]{2,1,0:T(8,128)} %fusion.1) | copy-start | bytes 1572868
  122.1 5.2 %copy-start.7 = (f32[1,32,4096]{2,1,0:T(8,128)S(1)}, f32[1,32,4096]{2,1,0:T(8,128)}, u32[]{:S(2)}) copy-start(f32[1,32,4096]{2,1,0:T(8,128)} %all-reduce.5.cloned.1.call-done) | copy-start | bytes 1572868
  128.9 117.8 %all-reduce.9.cloned.1.call-start = ((), (), s32[]{:S(2)}) async-start(), calls=%async_computation.4 | async-start | bytes 1048576 | tf_op jit(solution)/shard_map/psum | solution.py:106
  185.6 5.2 %copy-start.2 = (bf16[384,4096]{1,0:T(8,128)(2,1)S(1)}, bf16[384,4096]{1,0:T(8,128)(2,1)}, u32[]{:S(2)}) copy-start(bf16[384,4096]{1,0:T(8,128)(2,1)} %copy-done) | copy-start | bytes 9437188
  185.6 5.2 %copy-start.4 = (f32[1,32,4096]{2,1,0:T(8,128)S(1)}, f32[1,32,4096]{2,1,0:T(8,128)}, u32[]{:S(2)}) copy-start(f32[1,32,4096]{2,1,0:T(8,128)} %fusion.7) | copy-start | bytes 1572868
  185.6 5.2 %copy-start.6 = (f32[1,32,4096]{2,1,0:T(8,128)S(1)}, f32[1,32,4096]{2,1,0:T(8,128)}, u32[]{:S(2)}) copy-start(f32[1,32,4096]{2,1,0:T(8,128)} %all-reduce.7.cloned.1.call-done) | copy-start | bytes 1572868
  190.4 2.1 copy-start.13
  192.4 79.9 %reduce-scatter.2.cloned.1.call-start = ((), (), s32[]{:S(2)}) async-start(), calls=%async_computation.5 | async-start | bytes 655360 | tf_op jit(solution)/shard_map/reduce_scatter | solution.py:119
  251.0 56.6 %all-reduce.11.cloned.1.call-start = ((), (), s32[]{:S(2)}) async-start(), calls=%async_computation.6 | async-start | bytes 131072 | tf_op jit(solution)/shard_map/psum | solution.py:131
  273.3 35.9 %copy-start.12 = (f32[32,1024]{1,0:T(8,128)}, f32[32,1024]{1,0:T(8,128)S(1)}, u32[]{:S(2)}) copy-start(f32[32,1024]{1,0:T(8,128)S(1)} %broadcast_divide_fusion) | copy-start | bytes 393220
Sparse Core Ops, SparseCore 0:
  61.4 58.2 all-reduce.4
  129.0 54.1 all-reduce.6
  192.5 54.1 all-reduce.8
  251.2 21.1 reduce-scatter.1
  275.1 32.5 all-reduce.10
where the time goes:
time: 316 us
  waiting for transfers between devices  211 us (67%)
  blocking collectives  25.1 us (8%)
  matrix products  24 us (8%)
  other arithmetic  20.6 us (7%)
  between operations  17.4 us (6%)
  local copies, waits for them, and re-layouts  15.9 us (5%)
    psum x3, waiting for transfers between devices, per_device(): mean_value = lax.psum(stacked, 'tm') / shards  157 us
    psum x1, waiting for transfers between devices, per_device(): predicted_output = lax.psum(partial_result, 'boot')  33.1 us
    reduce_scatter x1, waiting for transfers between devices, per_device(): summed = lax.psum_scatter(weighted, 'boot', scatter_dimension=1, tiled=True)  21.2 us
    psum x1, blocking collectives, per_device(): power = lax.psum(jnp.sum(values * values, axis=0), 'tm')  15.2 us
    gather x4, local copies, waits for them, and re-layouts, bootstrap_rows(): jnp.take(window, times + LAGS - 1 - delay_step, axis=0)  10.8 us
    all_to_all x1, blocking collectives, per_device(): lax.all_to_all(support, 'boot', split_axis=0, concat_axis=1, tiled=True)  9.94 us
    dot_general x3, matrix products, per_device(): jnp.einsum('brf,bcf->brc', target.astype(jnp.bfloat16), design, preferred...  7.84 us
  transfers between devices with their start and end apart: 6, of which 5 were waited for; matrix products, arithmetic and copies ran while one was open for 1% of the time, Pallas kernels for 0%

commit v1 on v0

--- a/solution.py
+++ b/solution.py
@@ -13,6 +13,15 @@
 ridge_weight = 4.0
 shrink_level = 0.75
 epsilon = 1e-05
+
+
+def add_in_pairs(x, mesh_axis):
+    count = lax.axis_size(mesh_axis)
+    result, far = (x, 1)
+    while far < count:
+        result = result + lax.ppermute(result, mesh_axis, [(i, i ^ far) for i in range(count)])
+        far = 2 * far
+    return result
 
 
 def passed_along(block, axis, distance):
@@ -128,7 +137,7 @@
         (((1,), (1,)), ((), ())),
         preferred_element_type=jnp.float32,
     )
-    predicted_output = lax.psum(partial_result, "boot")
+    predicted_output = add_in_pairs(partial_result, "boot")
     residual = scaled_input[:, :RESPONSE_COUNT].astype(jnp.float32).T - predicted_output
     return (averaged, residual)
 

time: 316 us -> 291 us (0.921)
  waiting for transfers between devices: 211 us -> 187 us
    psum x1 -> x0, waiting for transfers between devices: 33.1 us -> none  [per_device(): predicted_output = lax.psum(partial_result, 'boot')]
    ppermute x0 -> x2, waiting for transfers between devices: none -> 8.85 us  [add_in_pairs(): lax.ppermute(result, mesh_axis, [(i, i ^ far) for i in range(count)])]
  transfers between devices with their start and end apart: 6 -> 7, of which waited for: 5 -> 6; matrix products, arithmetic and copies ran while one was open for 1% -> 1% of each run, Pallas kernels for 0% -> 0%
where the time goes in v1:
time: 291 us
  waiting for transfers between devices  187 us (64%)
  blocking collectives  25.1 us (9%)
  matrix products  23.4 us (8%)
  other arithmetic  19.7 us (7%)
  between operations  17.4 us (6%)
  local copies, waits for them, and re-layouts  15.9 us (5%)
    psum x3, waiting for transfers between devices, per_device(): mean_value = lax.psum(stacked, 'tm') / shards  157 us
    reduce_scatter x1, waiting for transfers between devices, per_device(): summed = lax.psum_scatter(weighted, 'boot', scatter_dimension=1, tiled=True)  21.3 us
    psum x1, blocking collectives, per_device(): power = lax.psum(jnp.sum(values * values, axis=0), 'tm')  15.2 us
    gather x4, local copies, waits for them, and re-layouts, bootstrap_rows(): jnp.take(window, times + LAGS - 1 - delay_step, axis=0)  10.8 us
    all_to_all x1, blocking collectives, per_device(): lax.all_to_all(support, 'boot', split_axis=0, concat_axis=1, tiled=True)  9.94 us
    ppermute x2, waiting for transfers between devices, add_in_pairs(): lax.ppermute(result, mesh_axis, [(i, i ^ far) for i in range(count)])  8.85 us
    dot_general x3, matrix products, per_device(): jnp.einsum('brf,bcf->brc', target.astype(jnp.bfloat16), design, preferred...  7.84 us
  transfers between devices with their start and end apart: 7, of which 6 were waited for; matrix products, arithmetic and copies ran while one was open for 1% of the time, Pallas kernels for 0%

profile of v1, /device:TPU:0, one launch (start us, length us, event | category | flops | bytes accessed | tf_op | source)
XLA Modules:
  0.0 290.8 jit_solution(8321471493580207820)
XLA Ops:
  7.2 1.5 copy.24
  9.0 15.2 %psum.28 = f32[1024]{0:T(1024)S(1)} all-reduce(f32[1024]{0:T(1024)S(1)} %fusion.9), channel_id=1, replica_groups=mesh['boot'=4,'tm'=8] {'tm'}, use_global_device_ids=true, to_apply=%region_5.6 | all-reduce | flops 1024 | bytes 8192 | tf_op jit(solution)/shard_map/psum | solution.py:82
  24.6 1.3 collective-permute-start
  26.1 0.6 slice.12
  26.9 0.7 iota_compare_fusion
  27.6 0.7 fusion.114
  28.3 0.7 and_reduce_fusion.3
  29.1 0.7 copy-done.10
  29.8 0.7 pad_maximum_fusion
  30.5 0.6 copy.26
  31.1 2.7 gather_fusion.4
  33.8 2.7 gather_fusion.3
  36.5 2.7 gather_fusion.2
  39.2 2.7 gather_fusion.1
  41.9 2.7 fusion.38
  44.5 1.4 fusion.42
  45.9 0.9 fusion.8
  46.8 2.5 multiply_reduce_fusion
  50.7 1.4 gather_fusion
  52.1 2.7 convolution_multiply_fusion
  54.8 2.1 maximum_select_fusion.1
  56.9 1.0 convolution_multiply_fusion.4
  59.3 0.5 fusion.32
  59.7 1.5 fusion.1
  61.5 58.2 %all-reduce.4.cloned.1.call-done = f32[1,32,4096]{2,1,0:T(8,128)} async-done(((f32[1,32,4096]{2,1,0:T(8,128)}), f32[1,32,4096]{2,1,0:T(8,128)}) %all-reduce.4.cloned.1.call-update) | async-done | bytes 524304 | tf_op jit(solution)/shard_map/psum | solution.py:115
  119.7 1.1 multiply_reduce_fusion.3
  120.8 0.7 sqrt_reduce_fusion.2
  122.2 3.4 %convolution_multiply_fusion.3 = f32[32,384]{1,0:T(8,128)S(1)} fusion(bf16[384,4096]{1,0:T(8,128)(2,1)} %copy-done.3, f32[1,32,4096]{2,1,0:T(8,128)} %fusion.1, f32[1,32,4096]{2,1,0:T(8,128)} %all-reduce.4.cloned.1.call-done, f32[32,4096]{1,0:T(8,128)S(1)} %convolution_multiply_fusion, f32[4096]{0:T(1024)S(1)} %divide_multiply_fusion.2), kind=kOutput, calls=%fused_computation.31 | convolution fusion | flops 101462016 | bytes 4784128 | tf_op jit(solution)/shard_map/brf,bcf->brc/dot_general | solution.py:101
  126.9 0.5 fusion.33
  127.4 1.5 fusion.7
  129.0 54.2 %all-reduce.6.cloned.1.call-done = f32[1,32,4096]{2,1,0:T(8,128)} async-done(((f32[1,32,4096]{2,1,0:T(8,128)}), f32[1,32,4096]{2,1,0:T(8,128)}) %all-reduce.6.cloned.1.call-update) | async-done | bytes 524304 | tf_op jit(solution)/shard_map/psum | solution.py:115
  183.2 1.1 multiply_reduce_fusion.2
  184.3 0.7 sqrt_reduce_fusion.1
  185.7 3.4 %convolution_multiply_fusion.2 = f32[32,384]{1,0:T(8,128)S(1)} fusion(bf16[384,4096]{1,0:T(8,128)(2,1)} %copy-done.3, f32[1,32,4096]{2,1,0:T(8,128)} %fusion.7, f32[1,32,4096]{2,1,0:T(8,128)} %all-reduce.6.cloned.1.call-done, f32[32,4096]{1,0:T(8,128)S(1)} %convolution_multiply_fusion, f32[4096]{0:T(1024)S(1)} %divide_multiply_fusion.1), kind=kOutput, calls=%fused_computation.30 | convolution fusion | flops 101462016 | bytes 4784128 | tf_op jit(solution)/shard_map/brf,bcf->brc/dot_general | solution.py:101
  190.4 0.5 fusion.34
  190.9 1.5 fusion.4
  192.6 9.9 %all_to_all.13 = s32[4,1,1024]{2,1,0:T(1,128)S(1)} all-to-all(s32[4,1,1024]{2,1,0:T(1,128)S(1)} %all_to_all.10), channel_id=1, replica_groups=mesh['boot'=4,'tm'=8] {'boot'}, dimensions={0} | all-to-all | bytes 32768 | tf_op jit(solution)/shard_map/all_to_all | solution.py:124
  202.5 44.2 %all-reduce.8.cloned.1.call-done = f32[1,32,4096]{2,1,0:T(8,128)} async-done(((f32[1,32,4096]{2,1,0:T(8,128)}), f32[1,32,4096]{2,1,0:T(8,128)}) %all-reduce.8.cloned.1.call-update) | async-done | bytes 524304 | tf_op jit(solution)/shard_map/psum | solution.py:115
  246.7 1.1 multiply_reduce_fusion.1
  247.8 0.6 sqrt_reduce_fusion
  249.1 1.9 multiply_bitcast_fusion
  251.1 21.3 %reduce-scatter.2.cloned.1.call-done = f32[32,1024]{1,0:T(8,128)} async-done(((f32[32,4096]{1,0:T(8,128)}), f32[32,1024]{1,0:T(8,128)}) %reduce-scatter.2.cloned.1.call-update) | async-done | bytes 131088 | tf_op jit(solution)/shard_map/reduce_scatter | solution.py:128
  272.4 0.9 broadcast_divide_fusion
  273.3 0.7 fusion.36
  274.0 4.3 %collective-permute-done.1 = f32[32,512]{1,0:T(8,128)S(1)} collective-permute-done((f32[32,512]{1,0:T(8,128)S(1)}, f32[32,512]{1,0:T(8,128)S(1)}, u32[]{:S(2)}, u32[]{:S(2)}) %collective-permute-start.1) | collective-permute-done | bytes 65568 | tf_op jit(solution)/shard_map/ppermute | solution.py:22
  278.3 0.8 collective-permute-start.2
  279.1 4.6 %collective-permute-done.2 = f32[32,512]{1,0:T(8,128)S(1)} collective-permute-done((f32[32,512]{1,0:T(8,128)S(1)}, f32[32,512]{1,0:T(8,128)S(1)}, u32[]{:S(2)}, u32[]{:S(2)}) %collective-permute-start.2) | collective-permute-done | bytes 65568 | tf_op jit(solution)/shard_map/ppermute | solution.py:22
  283.7 0.6 bitcast_subtract_fusion
  (75 shorter events, 5.9 us)
Async XLA Ops:
  7.2 18.8 %copy-start.15 = (s32[1,6]{1,0:T(1,128)S(1)}, s32[1,6]{1,0:T(1,128)}, u32[]{:S(2)}) copy-start(s32[1,6]{1,0:T(1,128)} %param.8) | copy-start | bytes 76
  7.2 19.6 %copy-start.14 = (s32[1,6]{1,0:T(1,128)S(1)}, s32[1,6]{1,0:T(1,128)}, u32[]{:S(2)}) copy-start(s32[1,6]{1,0:T(1,128)} %param.7) | copy-start | bytes 76
  7.2 112.5 %all-reduce.4.cloned.1.call-start = ((), (), s32[]{:S(2)}) async-start(), calls=%async_computation.2 | async-start | bytes 1048576 | tf_op jit(solution)/shard_map/psum | solution.py:115
  24.6 4.4 %collective-permute-start = (bf16[4,1024]{0,1:T(8,128)(2,1)S(1)}, bf16[4,1024]{0,1:T(8,128)(2,1)S(1)}, u32[]{:S(2)}, u32[]{:S(2)}) collective-permute-start(bf16[4,1024]{0,1:T(8,128)(2,1)S(1)} %slice.26), channel_id=1, source_target_pairs={{0,1},{1,2},{2,3},{3,4},{4,5},{5,6},{6,7},{8,9},{9,10},{10,11},{11... | collective-permute-start | bytes 24584 | tf_op jit(solution)/shard_map/ppermute | solution.py:30
  29.1 0.7 copy-start.10
  41.9 2.7 copy-start.8
  41.9 2.7 copy-start.9
  46.8 2.5 copy-start.3
  46.8 3.4 %copy-start.11 = (bf16[4,1024]{0,1:T(8,128)(2,1)S(1)}, bf16[4,1024]{0,1:T(8,128)(2,1)}, u32[]{:S(2)}) copy-start(bf16[4,1024]{0,1:T(8,128)(2,1)} %copy-done.10) | copy-start | bytes 24580
  56.9 2.8 copy-start
  61.3 121.9 %all-reduce.6.cloned.1.call-start = ((), (), s32[]{:S(2)}) async-start(), calls=%async_computation.3 | async-start | bytes 1048576 | tf_op jit(solution)/shard_map/psum | solution.py:115
  122.1 5.2 %copy-start.1 = (bf16[384,4096]{1,0:T(8,128)(2,1)S(1)}, bf16[384,4096]{1,0:T(8,128)(2,1)}, u32[]{:S(2)}) copy-start(bf16[384,4096]{1,0:T(8,128)(2,1)} %copy-done) | copy-start | bytes 9437188
  122.1 5.2 %copy-start.5 = (f32[1,32,4096]{2,1,0:T(8,128)S(1)}, f32[1,32,4096]{2,1,0:T(8,128)}, u32[]{:S(2)}) copy-start(f32[1,32,4096]{2,1,0:T(8,128)} %fusion.1) | copy-start | bytes 1572868
  122.2 5.2 %copy-start.7 = (f32[1,32,4096]{2,1,0:T(8,128)S(1)}, f32[1,32,4096]{2,1,0:T(8,128)}, u32[]{:S(2)}) copy-start(f32[1,32,4096]{2,1,0:T(8,128)} %all-reduce.4.cloned.1.call-done) | copy-start | bytes 1572868
  128.9 117.8 %all-reduce.8.cloned.1.call-start = ((), (), s32[]{:S(2)}) async-start(), calls=%async_computation.4 | async-start | bytes 1048576 | tf_op jit(solution)/shard_map/psum | solution.py:115
  185.7 5.2 %copy-start.2 = (bf16[384,4096]{1,0:T(8,128)(2,1)S(1)}, bf16[384,4096]{1,0:T(8,128)(2,1)}, u32[]{:S(2)}) copy-start(bf16[384,4096]{1,0:T(8,128)(2,1)} %copy-done) | copy-start | bytes 9437188
  185.7 5.2 %copy-start.4 = (f32[1,32,4096]{2,1,0:T(8,128)S(1)}, f32[1,32,4096]{2,1,0:T(8,128)}, u32[]{:S(2)}) copy-start(f32[1,32,4096]{2,1,0:T(8,128)} %fusion.7) | copy-start | bytes 1572868
  185.7 5.2 %copy-start.6 = (f32[1,32,4096]{2,1,0:T(8,128)S(1)}, f32[1,32,4096]{2,1,0:T(8,128)}, u32[]{:S(2)}) copy-start(f32[1,32,4096]{2,1,0:T(8,128)} %all-reduce.6.cloned.1.call-done) | copy-start | bytes 1572868
  190.4 2.1 copy-start.13
  192.5 79.9 %reduce-scatter.2.cloned.1.call-start = ((), (), s32[]{:S(2)}) async-start(), calls=%async_computation.5 | async-start | bytes 655360 | tf_op jit(solution)/shard_map/reduce_scatter | solution.py:128
  273.3 11.0 %copy-start.12 = (f32[32,1024]{1,0:T(8,128)}, f32[32,1024]{1,0:T(8,128)S(1)}, u32[]{:S(2)}) copy-start(f32[32,1024]{1,0:T(8,128)S(1)} %broadcast_divide_fusion) | copy-start | bytes 393220
  274.0 4.3 %collective-permute-start.1 = (f32[32,512]{1,0:T(8,128)S(1)}, f32[32,512]{1,0:T(8,128)S(1)}, u32[]{:S(2)}, u32[]{:S(2)}) collective-permute-start(f32[32,512]{1,0:T(8,128)S(1)} %fusion.36), channel_id=1, source_target_pairs={{0,8},{8,0},{16,24},{24,16},{1,9},{9,1},{17,25},{25,17},{2,10},{10... | collective-permute-start | bytes 196616 | tf_op jit(solution)/shard_map/ppermute | solution.py:22
  278.3 5.4 %collective-permute-start.2 = (f32[32,512]{1,0:T(8,128)S(1)}, f32[32,512]{1,0:T(8,128)S(1)}, u32[]{:S(2)}, u32[]{:S(2)}) collective-permute-start(f32[32,512]{1,0:T(8,128)S(1)} %add.410), channel_id=1, source_target_pairs={{0,16},{8,24},{16,0},{24,8},{1,17},{9,25},{17,1},{25,9},{2,18},{10... | collective-permute-start | bytes 196616 | tf_op jit(solution)/shard_map/ppermute | solution.py:22
Sparse Core Ops, SparseCore 0:
  61.4 58.2 all-reduce.3
  129.1 54.1 all-reduce.5
  192.6 54.0 all-reduce.7
  251.2 21.1 reduce-scatter.1
